TPU v7x, 128 devices: a whole 4x4x4 slice. The times are simulated.
128 devices in a mesh: tm: 16 (over x_hi, y, core), row: 2 (over x_lo), col: 4 (over z).
Axes of the slice: x: 4 (x_hi: 2, x_lo: 2; x = x_hi * 2 + x_lo), y: 4, z: 4, core: 2. Of those that a mesh axis runs over, the one named last changes fastest.
Arguments:
- coarse: bfloat16 [64, 16, 64, 256], P('tm', 'row', 'col'), may hold values from -6 to 6
- kernels: bfloat16 [3, 3, 3, 3, 256, 256], replicated, may hold values from -0.078125 to 0.078125
- biases: float32 [3, 256], replicated, may hold values from -3 to 3
Outputs:
- decoded: bfloat16 [64, 32, 128, 256], P('tm', 'row', 'col')
All inputs are finite; a program needn't handle non-finite values.
Results may differ from a plain program's by a relative error of at most 0.0031.
Values may be sent and summed in bfloat16 or wider, within the bound.
A program may use at most 128 MiB of HBM per device.

v0:
```python
import functools

import jax
import jax.numpy as jnp
from jax import lax
from jax.experimental import pallas as pl
from jax.experimental.pallas import tpu as pltpu
from jax.sharding import PartitionSpec as P

F32 = jnp.float32
BF16 = jnp.bfloat16
MESH = pl.DeviceIdType.MESH
C = 256
TAP = 9


def silu(v):
    return v * (0.5 + 0.5 * jnp.tanh(0.5 * v))


def joined(ref, *at):
    *outer, rows = at
    return jnp.concatenate([ref[(*outer, half, rows)] for half in range(2)], axis=-1)


def parted(value, ref, *at):
    *outer, rows = at
    for half in range(2):
        ref[(*outer, half, rows)] = value[:, 128 * half:128 * half + 128]


def rounded(v):
    return v.astype(BF16).astype(F32)


def kernel(sizes, coarse_hbm, kernels_hbm, bias_ref, out_hbm,
           wraw, u0, u1, raw, cells, cell_cols, cell_stage, diffs,
           act1, act2, cols1, cols2, stage1, stage2, v1, v2, acc, scr, oscr, obuf,
           in_sem, w_sem, out_sem, c_send, c_recv, h_send, h_recv):
    tms, rows, ncols = sizes
    tm, row, col = lax.axis_index("tm"), lax.axis_index("row"), lax.axis_index("col")
    other = 1 - row

    coarse_in = pltpu.make_async_copy(coarse_hbm, raw, in_sem)
    coarse_in.start()
    w_in = []
    for layer in range(3):
        for t in range(3):
            copy = pltpu.make_async_copy(
                kernels_hbm.at[layer, pl.ds(t * TAP, TAP)], wraw.at[layer, pl.ds(t * TAP, TAP)], w_sem.at[layer, t])
            copy.start()
            w_in.append(copy)

    cells[...] = jnp.zeros_like(cells)
    cell_cols[...] = jnp.zeros_like(cell_cols)
    cols1[...] = jnp.zeros_like(cols1)
    cols2[...] = jnp.zeros_like(cols2)
    for act in (act1, act2):
        edge = jnp.zeros((2, act.shape[1], 1, 16, C), BF16)
        act[:, :, 0:1] = edge
        act[:, :, 17:18] = edge

    peers = [(dt, dr, dc) for dt in range(3) for dr in range(2) for dc in (-1, 0, 1) if (dt, dr, dc) != (0, 0, 0)]

    def exists(dt, dc, sign):
        ok = True
        if dt:
            ok = (tm + sign * dt >= 0) & (tm + sign * dt < tms)
        if dc:
            near = (col + sign * dc >= 0) & (col + sign * dc < ncols)
            ok = near if ok is True else ok & near
        return ok

    def when(cond, body):
        if cond is True:
            body()
        else:
            pl.when(cond)(body)

    def place(dt, dr, dc, sign):
        return (tm + sign * dt, other if dr else row, col + sign * dc)

    barrier = pltpu.get_barrier_semaphore()
    for dt, dr, dc in peers:
        def greet(dt=dt, dr=dr, dc=dc):
            pl.semaphore_signal(barrier, inc=1, device_id=place(dt, dr, dc, -1), device_id_type=MESH)
        when(exists(dt, dc, -1), greet)

    coarse_in.wait()
    for f in range(4):
        acted = silu(raw[f].astype(F32)).astype(BF16)
        cells[6 + f, 1:9] = acted.reshape(8, 16, C)
        parted(acted.astype(F32), scr, 0, pl.ds(0, 128))
        cell_stage[0, f] = joined(scr, 0, pl.ds(15, 8, stride=16))
        cell_stage[1, f] = joined(scr, 0, pl.ds(0, 8, stride=16))

    ahead = jnp.minimum(tms - 1 - tm, 2)
    beside = jnp.minimum(col, 1) + jnp.minimum(ncols - 1 - col, 1)
    pl.semaphore_wait(barrier, (1 + ahead) * 2 * (1 + beside) - 1)

    groups = [(0, 0, 4, 6), (1, 2, 2, 4), (1, 0, 2, 2), (2, 2, 2, 0)]

    def cell_copy(g, kind):
        dt, src, count, dst = groups[g]
        if kind == 0:
            s, d, dr, dc = cells.at[pl.ds(6 + src, count), pl.ds(1, 8)], cells.at[pl.ds(dst, count), pl.ds(1, 8)], 0, 0
        elif kind == 1:
            s, d, dr, dc = cells.at[pl.ds(6 + src, count), 8 - 7 * row], cells.at[pl.ds(dst, count), 9 * row], 1, 0
        else:
            side = kind % 2
            dc = 1 - 2 * side
            if kind < 4:
                s, d, dr = cell_stage.at[side, pl.ds(src, count)], cell_cols.at[side, pl.ds(dst, count), pl.ds(8, 8)], 0
            else:
                at = pl.multiple_of(16 * row, 8)
                s, d, dr = cell_stage.at[side, pl.ds(src, count)], cell_cols.at[side, pl.ds(dst, count), pl.ds(at, 8)], 1
        copy = pltpu.make_async_remote_copy(
            src_ref=s, dst_ref=d, send_sem=c_send.at[g, kind], recv_sem=c_recv.at[g, kind],
            device_id=place(dt, dr, dc, 1), device_id_type=MESH)
        return copy, exists(dt, dc, 1), exists(dt, dc, -1)

    def cell_kinds(g):
        return range(1 if groups[g][0] == 0 else 0, 6)

    for g in range(4):
        for kind in cell_kinds(g):
            copy, there, _ = cell_copy(g, kind)
            when(there, copy.start)

    def cells_arrived(g):
        for kind in cell_kinds(g):
            copy, _, there = cell_copy(g, kind)
            when(there, copy.wait_recv)

    def halo_copy(layer, pair, kind):
        act, cols, stage = (act1, cols1, stage1) if layer == 1 else (act2, cols2, stage2)
        two = pl.ds(2 * pair, 2)
        if kind == 0:
            s, d, dr, dc = act.at[:, two, 16 - 15 * row], act.at[:, two, 17 * row], 1, 0
        else:
            side = (kind - 1) % 2
            dc = 1 - 2 * side
            if kind < 3:
                s, d, dr = stage.at[side, two], cols.at[side, two, pl.ds(8, 16)], 0
            else:
                s = stage.at[side, two, pl.ds(pl.multiple_of(8 * other, 8), 8)]
                d, dr = cols.at[side, two, pl.ds(pl.multiple_of(24 * row, 8), 8)], 1
        copy = pltpu.make_async_remote_copy(
            src_ref=s, dst_ref=d, send_sem=h_send.at[layer - 1, pair, kind], recv_sem=h_recv.at[layer - 1, pair, kind],
            device_id=place(0, dr, dc, 1), device_id_type=MESH)
        return copy, exists(0, dc, 1), exists(0, dc, -1)

    def send_halos(layer, pair):
        for kind in range(5):
            copy, there, _ = halo_copy(layer, pair, kind)
            when(there, copy.start)

    def halos_arrived(layer, pair):
        for kind in range(5):
            copy, _, there = halo_copy(layer, pair, kind)
            when(there, copy.wait_recv)

    def weights_0(t):
        w_in[t].wait()

        def chunk(i, carry):
            at = pl.ds(pl.multiple_of(i * 16, 16), 16)
            taps = [wraw[0, t * TAP + m, at, :].astype(F32) for m in range(9)]
            to = pl.ds(pl.multiple_of(t * C + i * 16, 16), 16)
            across = []
            for y in range(3):
                a, b, c = taps[3 * y:3 * y + 3]
                across.append([a, a + b + c, c])
            for kx in range(3):
                a, b, c = across[0][kx], across[1][kx], across[2][kx]
                for ky, value in enumerate((a, a + b + c, c)):
                    u0[ky * 3 + kx, to, :] = value.astype(BF16)
            return carry
        lax.fori_loop(0, 16, chunk, 0)

    def weights(layer):
        for t in range(3):
            w_in[3 * layer + t].wait()

        def chunk(i, carry):
            m, part = i // 4, i % 4
            at = pl.ds(pl.multiple_of(part * 64, 64), 64)
            to = pl.ds(pl.multiple_of(i * 64, 64), 64)
            a = wraw[layer, 3 * m, at, :]
            c = wraw[layer, 3 * m + 2, at, :]
            half = 0.5 * (a.astype(F32) + c.astype(F32))
            b = 0.5 * wraw[layer, 3 * m + 1, at, :].astype(F32)
            u1[layer - 1, 0, to, :] = a
            u1[layer - 1, 1, to, :] = (half + b).astype(BF16)
            u1[layer - 1, 2, to, :] = (half - b).astype(BF16)
            u1[layer - 1, 3, to, :] = c
            return carry
        lax.fori_loop(0, 36, chunk, 0)

    def build_diffs(first, count):
        def frame(f, carry):
            c = cells[f].astype(F32).reshape(160, C)
            every = pl.ds(0, 160)
            parted(pltpu.roll(c, 1, 0), scr, 0, every)
            parted(cell_cols[0, f, 7:17, :], scr, 0, pl.ds(0, 10, stride=16))
            parted(pltpu.roll(c, 159, 0), scr, 1, every)
            parted(cell_cols[1, f, 7:17, :], scr, 1, pl.ds(15, 10, stride=16))
            for kx, x in enumerate((joined(scr, 0, every) - c, c, joined(scr, 1, every) - c)):
                mid = x[16:144]
                diffs[kx, f] = (x[0:128] - mid).astype(BF16)
                diffs[3 + kx, f] = mid.astype(BF16)
                diffs[6 + kx, f] = (x[32:160] - mid).astype(BF16)
            return carry
        lax.fori_loop(first, first + count, frame, 0)

    live = tm > 0

    def layer_0(pair):
        o = 2 * pair
        for m in range(9):
            lhs = jnp.concatenate([diffs[m, o + t:o + t + 2].reshape(256, C) for t in range(3)], axis=1)
            parted(jnp.dot(lhs, u0[m], preferred_element_type=F32), acc, m, pl.ds(0, 256))
        bias = bias_ref[0:1, :]

        def phases(at):
            p = [joined(acc, m, at) for m in range(9)]
            left, right = p[4] + p[3] + bias, p[4] + p[5] + bias
            out = [[left + (p[1] + p[0]), right + (p[1] + p[2])],
                   [left + (p[7] + p[6]), right + (p[7] + p[8])]]
            out = [[silu(v) for v in line] for line in out]
            if pair < 2:
                out = [[jnp.where(live, v, 0.0) for v in line] for line in out]
            return out

        for side, x in ((0, 15), (1, 0)):
            edge = phases(pl.ds(x, 16, stride=16))
            for py in range(2):
                parted(rounded(edge[py][1 - side]), scr, 0, pl.ds(py, 16, stride=2))
            for f in range(2):
                stage1[side, o + f] = joined(scr, 0, pl.ds(16 * f, 16))
        for f in range(2):
            def line(i, carry, f=f):
                out = phases(pl.ds(pl.multiple_of(f * 128 + i * 16, 16), 16))
                for py in range(2):
                    for px in range(2):
                        act1[px, o + f, 1 + 2 * i + py] = out[py][px].astype(BF16)
                return carry
            lax.fori_loop(0, 8, line, 0, unroll=2)
        send_halos(1, pair)

    def build_v(layer, pair):
        act, cols, v = (act1, cols1, v1) if layer == 1 else (act2, cols2, v2)
        halos_arrived(layer, pair)
        for f in (2 * pair, 2 * pair + 1):
            e = act[0, f].astype(F32).reshape(288, C)
            o = act[1, f].astype(F32).reshape(288, C)
            every = pl.ds(0, 288)
            parted(pltpu.roll(o, 1, 0), scr, 0, every)
            parted(cols[0, f, 7:25, :], scr, 0, pl.ds(0, 18, stride=16))
            parted(pltpu.roll(e, 287, 0), scr, 1, every)
            parted(cols[1, f, 7:25, :], scr, 1, pl.ds(15, 18, stride=16))
            v[0, f] = (joined(scr, 0, every) - o).astype(BF16)
            v[1, f] = (e + o).astype(BF16)
            v[2, f] = (o - e).astype(BF16)
            v[3, f] = (e - joined(scr, 1, every)).astype(BF16)

    def products(layer, pair):
        v = v1 if layer == 1 else v2
        o = 2 * pair
        for k in range(4):
            lhs = jnp.concatenate(
                [v[k, o + t:o + t + 2, 16 * y:16 * y + 256].reshape(512, C) for t in range(3) for y in range(3)], axis=1)
            parted(jnp.dot(lhs, u1[layer - 1, k], preferred_element_type=F32), acc, k, pl.ds(0, 512))

    def outputs(layer, at):
        bias = bias_ref[layer:layer + 1, :]
        m = [joined(acc, k, at) for k in range(4)]
        return (m[0] + m[1]) + (m[2] + bias), (m[1] - m[2]) - (m[3] - bias)

    def layer_1(pair):
        products(1, pair)
        o = 2 * pair

        def acted(at):
            out = [silu(v) for v in outputs(1, at)]
            if pair < 1:
                out = [jnp.where(live, v, 0.0) for v in out]
            return out

        for side, x in ((0, 15), (1, 0)):
            value = rounded(acted(pl.ds(x, 32, stride=16))[1 - side])
            for f in range(2):
                stage2[side, o + f] = value[16 * f:16 * f + 16]
        for f in range(2):
            def line(i, carry, f=f):
                e, o_ = acted(pl.ds(pl.multiple_of(f * 256 + i * 32, 32), 32))
                two = pl.ds(1 + 2 * i, 2)
                act2[0, o + f, two] = e.astype(BF16).reshape(2, 16, C)
                act2[1, o + f, two] = o_.astype(BF16).reshape(2, 16, C)
                return carry
            lax.fori_loop(0, 8, line, 0, unroll=2)
        send_halos(2, pair)

    def layer_2(pair):
        products(2, pair)
        for f in range(2):
            def line(i, carry, f=f):
                e, o_ = outputs(2, pl.ds(pl.multiple_of(f * 256 + i * 32, 32), 32))
                up = raw[2 * pair + f, pl.ds(pl.multiple_of(i * 16, 16), 16), :].astype(F32)
                up = jnp.concatenate([up, up], axis=0)
                for lane in range(2):
                    half = slice(128 * lane, 128 * lane + 128)
                    oscr[lane, pl.ds(0, 32, stride=2), :] = (up + e)[:, half]
                    oscr[lane, pl.ds(1, 32, stride=2), :] = (up + o_)[:, half]
                    obuf[2 * pair + f, pl.ds(pl.multiple_of(i * 64, 64), 64), half] = oscr[lane].astype(BF16)
                return carry
            lax.fori_loop(0, 8, line, 0)
        copy = pltpu.make_async_copy(
            obuf.at[pl.ds(2 * pair, 2)], out_hbm.at[pl.ds(2 * pair, 2)], out_sem.at[pair])
        copy.start()
        return copy

    for t in range(3):
        weights_0(t)
    cells_arrived(0)
    build_diffs(6, 4)
    layer_0(3)
    weights(1)
    cells_arrived(1)
    build_diffs(4, 2)
    layer_0(2)
    cells_arrived(2)
    build_diffs(2, 2)
    layer_0(1)
    build_v(1, 3)
    build_v(1, 2)
    layer_1(2)
    cells_arrived(3)
    build_diffs(0, 2)
    layer_0(0)
    weights(2)
    build_v(1, 1)
    layer_1(1)
    build_v(1, 0)
    layer_1(0)
    build_v(2, 2)
    build_v(2, 1)
    out_b = layer_2(1)
    build_v(2, 0)
    out_a = layer_2(0)
    out_b.wait()
    out_a.wait()

    for g in range(4):
        for kind in cell_kinds(g):
            copy, there, _ = cell_copy(g, kind)
            when(there, copy.wait_send)
    for layer, pairs in ((1, 4), (2, 3)):
        for pair in range(pairs):
            for kind in range(5):
                copy, there, _ = halo_copy(layer, pair, kind)
                when(there, copy.wait_send)


def solution(mesh):
    sizes = tuple(mesh.shape[name] for name in ("tm", "row", "col"))

    def local(coarse, kernels, biases):
        any_space = pl.BlockSpec(memory_space=pl.ANY)
        decoded = pl.pallas_call(
            functools.partial(kernel, sizes),
            out_shape=jax.ShapeDtypeStruct((4, 512, C), BF16),
            in_specs=[any_space, any_space, pl.BlockSpec(memory_space=pltpu.VMEM)],
            out_specs=any_space,
            scratch_shapes=[
                pltpu.VMEM((3, 27, C, C), BF16),
                pltpu.VMEM((9, 3 * C, C), BF16),
                pltpu.VMEM((2, 4, 9 * C, C), BF16),
                pltpu.VMEM((4, 128, C), BF16),
                pltpu.VMEM((10, 10, 16, C), BF16),
                pltpu.VMEM((2, 10, 24, C), F32),
                pltpu.VMEM((2, 4, 8, C), F32),
                pltpu.VMEM((9, 10, 128, C), BF16),
                pltpu.VMEM((2, 8, 18, 16, C), BF16),
                pltpu.VMEM((2, 6, 18, 16, C), BF16),
                pltpu.VMEM((2, 8, 32, C), F32),
                pltpu.VMEM((2, 6, 32, C), F32),
                pltpu.VMEM((2, 8, 16, C), F32),
                pltpu.VMEM((2, 6, 16, C), F32),
                pltpu.VMEM((4, 8, 288, C), BF16),
                pltpu.VMEM((4, 6, 288, C), BF16),
                pltpu.VMEM((9, 2, 512, 128), F32),
                pltpu.VMEM((2, 2, 288, 128), F32),
                pltpu.VMEM((2, 64, 128), F32),
                pltpu.VMEM((4, 512, C), BF16),
                pltpu.SemaphoreType.DMA,
                pltpu.SemaphoreType.DMA((3, 3)),
                pltpu.SemaphoreType.DMA((2,)),
                pltpu.SemaphoreType.DMA((4, 6)),
                pltpu.SemaphoreType.DMA((4, 6)),
                pltpu.SemaphoreType.DMA((2, 4, 5)),
                pltpu.SemaphoreType.DMA((2, 4, 5)),
            ],
            compiler_params=pltpu.CompilerParams(
                collective_id=0, has_side_effects=True, vmem_limit_bytes=62 * 2**20),
        )(coarse.reshape(4, 128, C), kernels.reshape(3, 27, C, C), biases)
        return decoded.reshape(4, 16, 32, C)

    return jax.shard_map(
        local, mesh=mesh, in_specs=(P("tm", "row", "col", None), P(), P()),
        out_specs=P("tm", "row", "col", None), check_vma=False)
```

profile of v0, /device:TPU:4, one launch (start us, length us, event | category | flops | bytes accessed | tf_op | source)
XLA Modules:
  0.0 46.4 jit_solution(10663531082754224886)
XLA Ops:
  0.0 44.1 %shard_map.37 = bf16[4,512,256]{2,1,0:T(8,128)(2,1)} custom-call(bf16[4,128,256]{2,1,0:T(8,128)(2,1)} %bitcast.5, bf16[3,27,256,256]{3,2,1,0:T(8,128)(2,1)} %bitcast.3, f32[3,256]{1,0:T(4,128)} %bias_ref.1), custom_call_target="tpu_custom_call" | custom-call | tf_op jit(solution)/shard_map/pallas_call | solution.py:370
  44.1 2.3 %copy.5 = bf16[4,16,32,256]{3,2,1,0:T(8,128)(2,1)} copy(bf16[4,16,32,256]{3,2,1,0:T(8,128)(2,1)} %bitcast.4) | data formatting | bytes 2097152
where the time goes:
time: 46.5 us; the launch traced here: 46.4 us
  Pallas kernels  44.1 us (95%)
  local copies, waits for them, and re-layouts  2.26 us (5%)
    pallas_call x1, Pallas kernels, local(): pl.pallas_call(functools.partial(kernel, sizes), out_shape=jax.ShapeDtype...  44.1 us
    unnamed x1, local copies, waits for them, and re-layouts  2.26 us

commit v1 on v0

--- a/solution.py
+++ b/solution.py
@@ -33,10 +33,10 @@
     return v.astype(BF16).astype(F32)
 
 
-def kernel(sizes, coarse_hbm, kernels_hbm, bias_ref, out_hbm,
-           wraw, u0, u1, raw, cells, cell_cols, cell_stage, diffs,
-           act1, act2, cols1, cols2, stage1, stage2, v1, v2, acc, scr, oscr, obuf,
-           in_sem, w_sem, out_sem, c_send, c_recv, h_send, h_recv):
+def kernel(sizes, coarse_hbm, kernels_hbm, bias_ref, obuf,
+           wraw, u0, u1, raw, cells, cell_cols, cell_ends, cell_stage, cell_tips, diffs,
+           act1, act2, cols1, cols2, ends1, ends2, stage1, stage2, tips1, tips2, v1, v2, acc, scr, oscr,
+           in_sem, w_sem, c_send, c_recv, h_send, h_recv):
     tms, rows, ncols = sizes
     tm, row, col = lax.axis_index("tm"), lax.axis_index("row"), lax.axis_index("col")
     other = 1 - row
@@ -48,17 +48,9 @@
         for t in range(3):
             copy = pltpu.make_async_copy(
                 kernels_hbm.at[layer, pl.ds(t * TAP, TAP)], wraw.at[layer, pl.ds(t * TAP, TAP)], w_sem.at[layer, t])
-            copy.start()
             w_in.append(copy)
-
-    cells[...] = jnp.zeros_like(cells)
-    cell_cols[...] = jnp.zeros_like(cell_cols)
-    cols1[...] = jnp.zeros_like(cols1)
-    cols2[...] = jnp.zeros_like(cols2)
-    for act in (act1, act2):
-        edge = jnp.zeros((2, act.shape[1], 1, 16, C), BF16)
-        act[:, :, 0:1] = edge
-        act[:, :, 17:18] = edge
+    for copy in w_in[:3]:
+        copy.start()
 
     peers = [(dt, dr, dc) for dt in range(3) for dr in range(2) for dc in (-1, 0, 1) if (dt, dr, dc) != (0, 0, 0)]
 
@@ -86,79 +78,37 @@
             pl.semaphore_signal(barrier, inc=1, device_id=place(dt, dr, dc, -1), device_id_type=MESH)
         when(exists(dt, dc, -1), greet)
 
+    def clear(*refs):
+        for ref in refs:
+            ref[...] = jnp.zeros(ref.shape, ref.dtype)
+
+    clear(cells.at[:, 9 * row], act1.at[:, :, 17 * row], act2.at[:, :, 17 * row])
+    for side, edge in ((0, 0), (1, ncols - 1)):
+        @pl.when(col == edge)
+        def _(side=side):
+            clear(*(ref.at[side] for ref in (cell_cols, cell_ends, cols1, cols2, ends1, ends2)))
+
+    def clear_frames(first, count):
+        at = pl.ds(first, count)
+        clear(cells.at[at], cell_cols.at[:, at], cell_ends.at[:, at])
+
+    @pl.when(tm < 2)
+    def _():
+        clear_frames(0, 2)
+
+    @pl.when(tm < 1)
+    def _():
+        clear_frames(2, 4)
+
     coarse_in.wait()
     for f in range(4):
         acted = silu(raw[f].astype(F32)).astype(BF16)
         cells[6 + f, 1:9] = acted.reshape(8, 16, C)
         parted(acted.astype(F32), scr, 0, pl.ds(0, 128))
-        cell_stage[0, f] = joined(scr, 0, pl.ds(15, 8, stride=16))
-        cell_stage[1, f] = joined(scr, 0, pl.ds(0, 8, stride=16))
-
-    ahead = jnp.minimum(tms - 1 - tm, 2)
-    beside = jnp.minimum(col, 1) + jnp.minimum(ncols - 1 - col, 1)
-    pl.semaphore_wait(barrier, (1 + ahead) * 2 * (1 + beside) - 1)
-
-    groups = [(0, 0, 4, 6), (1, 2, 2, 4), (1, 0, 2, 2), (2, 2, 2, 0)]
-
-    def cell_copy(g, kind):
-        dt, src, count, dst = groups[g]
-        if kind == 0:
-            s, d, dr, dc = cells.at[pl.ds(6 + src, count), pl.ds(1, 8)], cells.at[pl.ds(dst, count), pl.ds(1, 8)], 0, 0
-        elif kind == 1:
-            s, d, dr, dc = cells.at[pl.ds(6 + src, count), 8 - 7 * row], cells.at[pl.ds(dst, count), 9 * row], 1, 0
-        else:
-            side = kind % 2
-            dc = 1 - 2 * side
-            if kind < 4:
-                s, d, dr = cell_stage.at[side, pl.ds(src, count)], cell_cols.at[side, pl.ds(dst, count), pl.ds(8, 8)], 0
-            else:
-                at = pl.multiple_of(16 * row, 8)
-                s, d, dr = cell_stage.at[side, pl.ds(src, count)], cell_cols.at[side, pl.ds(dst, count), pl.ds(at, 8)], 1
-        copy = pltpu.make_async_remote_copy(
-            src_ref=s, dst_ref=d, send_sem=c_send.at[g, kind], recv_sem=c_recv.at[g, kind],
-            device_id=place(dt, dr, dc, 1), device_id_type=MESH)
-        return copy, exists(dt, dc, 1), exists(dt, dc, -1)
-
-    def cell_kinds(g):
-        return range(1 if groups[g][0] == 0 else 0, 6)
-
-    for g in range(4):
-        for kind in cell_kinds(g):
-            copy, there, _ = cell_copy(g, kind)
-            when(there, copy.start)
-
-    def cells_arrived(g):
-        for kind in cell_kinds(g):
-            copy, _, there = cell_copy(g, kind)
-            when(there, copy.wait_recv)
-
-    def halo_copy(layer, pair, kind):
-        act, cols, stage = (act1, cols1, stage1) if layer == 1 else (act2, cols2, stage2)
-        two = pl.ds(2 * pair, 2)
-        if kind == 0:
-            s, d, dr, dc = act.at[:, two, 16 - 15 * row], act.at[:, two, 17 * row], 1, 0
-        else:
-            side = (kind - 1) % 2
-            dc = 1 - 2 * side
-            if kind < 3:
-                s, d, dr = stage.at[side, two], cols.at[side, two, pl.ds(8, 16)], 0
-            else:
-                s = stage.at[side, two, pl.ds(pl.multiple_of(8 * other, 8), 8)]
-                d, dr = cols.at[side, two, pl.ds(pl.multiple_of(24 * row, 8), 8)], 1
-        copy = pltpu.make_async_remote_copy(
-            src_ref=s, dst_ref=d, send_sem=h_send.at[layer - 1, pair, kind], recv_sem=h_recv.at[layer - 1, pair, kind],
-            device_id=place(0, dr, dc, 1), device_id_type=MESH)
-        return copy, exists(0, dc, 1), exists(0, dc, -1)
-
-    def send_halos(layer, pair):
-        for kind in range(5):
-            copy, there, _ = halo_copy(layer, pair, kind)
-            when(there, copy.start)
-
-    def halos_arrived(layer, pair):
-        for kind in range(5):
-            copy, _, there = halo_copy(layer, pair, kind)
-            when(there, copy.wait_recv)
+        for side, x in ((0, 15), (1, 0)):
+            edge = joined(scr, 0, pl.ds(x, 8, stride=16))
+            cell_stage[side, f] = edge.astype(BF16)
+            cell_tips[side, f] = jnp.where(row == 0, edge[7:8], edge[0:1])
 
     def weights_0(t):
         w_in[t].wait()
@@ -197,14 +147,93 @@
             return carry
         lax.fori_loop(0, 36, chunk, 0)
 
+    for t in range(3):
+        weights_0(t)
+
+    ahead = jnp.minimum(tms - 1 - tm, 2)
+    beside = jnp.minimum(col, 1) + jnp.minimum(ncols - 1 - col, 1)
+    pl.semaphore_wait(barrier, (1 + ahead) * 2 * (1 + beside) - 1)
+
+    groups = [(0, 0, 4, 6), (1, 2, 2, 4), (1, 0, 2, 2), (2, 2, 2, 0)]
+
+    def cell_copy(g, kind):
+        dt, src, count, dst = groups[g]
+        if kind == 0:
+            s, d, dr, dc = cells.at[pl.ds(6 + src, count), pl.ds(1, 8)], cells.at[pl.ds(dst, count), pl.ds(1, 8)], 0, 0
+        elif kind == 1:
+            s, d, dr, dc = cells.at[pl.ds(6 + src, count), 8 - 7 * row], cells.at[pl.ds(dst, count), 9 * row], 1, 0
+        else:
+            side = kind % 2
+            dc = 1 - 2 * side
+            if kind < 4:
+                s, d, dr = cell_stage.at[side, pl.ds(src, count)], cell_cols.at[side, pl.ds(dst, count)], 0
+            else:
+                s, d, dr = cell_tips.at[side, pl.ds(src, count)], cell_ends.at[side, pl.ds(dst, count)], 1
+        copy = pltpu.make_async_remote_copy(
+            src_ref=s, dst_ref=d, send_sem=c_send.at[g, kind], recv_sem=c_recv.at[g, kind],
+            device_id=place(dt, dr, dc, 1), device_id_type=MESH)
+        return copy, exists(dt, dc, 1), exists(dt, dc, -1)
+
+    def cell_kinds(g):
+        return range(1 if groups[g][0] == 0 else 0, 6)
+
+    for g in range(4):
+        for kind in cell_kinds(g):
+            copy, there, _ = cell_copy(g, kind)
+            when(there, copy.start)
+
+    for copy in w_in[3:]:
+        copy.start()
+
+    def cells_arrived(g):
+        for kind in cell_kinds(g):
+            copy, _, there = cell_copy(g, kind)
+            when(there, copy.wait_recv)
+
+    fine = {1: (act1, cols1, ends1, stage1, tips1), 2: (act2, cols2, ends2, stage2, tips2)}
+
+    def halo_copy(layer, pair, kind):
+        act, cols, ends, stage, tips = fine[layer]
+        two = pl.ds(2 * pair, 2)
+        if kind == 0:
+            s, d, dr, dc = act.at[:, two, 16 - 15 * row], act.at[:, two, 17 * row], 1, 0
+        else:
+            side = (kind - 1) % 2
+            dc = 1 - 2 * side
+            if kind < 3:
+                s, d, dr = stage.at[side, two], cols.at[side, two], 0
+            else:
+                s, d, dr = tips.at[side, two], ends.at[side, two], 1
+        copy = pltpu.make_async_remote_copy(
+            src_ref=s, dst_ref=d, send_sem=h_send.at[layer - 1, pair, kind], recv_sem=h_recv.at[layer - 1, pair, kind],
+            device_id=place(0, dr, dc, 1), device_id_type=MESH)
+        return copy, exists(0, dc, 1), exists(0, dc, -1)
+
+    def send_halos(layer, pair):
+        for kind in range(5):
+            copy, there, _ = halo_copy(layer, pair, kind)
+            when(there, copy.start)
+
+    def halos_arrived(layer, pair):
+        for kind in range(5):
+            copy, _, there = halo_copy(layer, pair, kind)
+            when(there, copy.wait_recv)
+
+    def put_edge(n, first, cols, ends, side, f):
+        height = cols.shape[2]
+        parted(cols[side, f].astype(F32), scr, n, pl.ds(first + 16, height, stride=16))
+        end = ends[side, f]
+        parted(jnp.where(row == 1, end, 0.0), scr, n, pl.ds(first, 1))
+        parted(jnp.where(row == 0, end, 0.0), scr, n, pl.ds(first + 16 * height + 16, 1))
+
     def build_diffs(first, count):
         def frame(f, carry):
             c = cells[f].astype(F32).reshape(160, C)
             every = pl.ds(0, 160)
             parted(pltpu.roll(c, 1, 0), scr, 0, every)
-            parted(cell_cols[0, f, 7:17, :], scr, 0, pl.ds(0, 10, stride=16))
+            put_edge(0, 0, cell_cols, cell_ends, 0, f)
             parted(pltpu.roll(c, 159, 0), scr, 1, every)
-            parted(cell_cols[1, f, 7:17, :], scr, 1, pl.ds(15, 10, stride=16))
+            put_edge(1, 15, cell_cols, cell_ends, 1, f)
             for kx, x in enumerate((joined(scr, 0, every) - c, c, joined(scr, 1, every) - c)):
                 mid = x[16:144]
                 diffs[kx, f] = (x[0:128] - mid).astype(BF16)
@@ -237,7 +266,9 @@
             for py in range(2):
                 parted(rounded(edge[py][1 - side]), scr, 0, pl.ds(py, 16, stride=2))
             for f in range(2):
-                stage1[side, o + f] = joined(scr, 0, pl.ds(16 * f, 16))
+                value = joined(scr, 0, pl.ds(16 * f, 16))
+                stage1[side, o + f] = value.astype(BF16)
+                tips1[side, o + f] = jnp.where(row == 0, value[15:16], value[0:1])
         for f in range(2):
             def line(i, carry, f=f):
                 out = phases(pl.ds(pl.multiple_of(f * 128 + i * 16, 16), 16))
@@ -249,16 +280,17 @@
         send_halos(1, pair)
 
     def build_v(layer, pair):
-        act, cols, v = (act1, cols1, v1) if layer == 1 else (act2, cols2, v2)
+        act, cols, ends, _, _ = fine[layer]
+        v = v1 if layer == 1 else v2
         halos_arrived(layer, pair)
         for f in (2 * pair, 2 * pair + 1):
             e = act[0, f].astype(F32).reshape(288, C)
             o = act[1, f].astype(F32).reshape(288, C)
             every = pl.ds(0, 288)
             parted(pltpu.roll(o, 1, 0), scr, 0, every)
-            parted(cols[0, f, 7:25, :], scr, 0, pl.ds(0, 18, stride=16))
+            put_edge(0, 0, cols, ends, 0, f)
             parted(pltpu.roll(e, 287, 0), scr, 1, every)
-            parted(cols[1, f, 7:25, :], scr, 1, pl.ds(15, 18, stride=16))
+            put_edge(1, 15, cols, ends, 1, f)
             v[0, f] = (joined(scr, 0, every) - o).astype(BF16)
             v[1, f] = (e + o).astype(BF16)
             v[2, f] = (o - e).astype(BF16)
@@ -290,7 +322,9 @@
         for side, x in ((0, 15), (1, 0)):
             value = rounded(acted(pl.ds(x, 32, stride=16))[1 - side])
             for f in range(2):
-                stage2[side, o + f] = value[16 * f:16 * f + 16]
+                line = value[16 * f:16 * f + 16]
+                stage2[side, o + f] = line.astype(BF16)
+                tips2[side, o + f] = jnp.where(row == 0, line[15:16], line[0:1])
         for f in range(2):
             def line(i, carry, f=f):
                 e, o_ = acted(pl.ds(pl.multiple_of(f * 256 + i * 32, 32), 32))
@@ -315,17 +349,12 @@
                     obuf[2 * pair + f, pl.ds(pl.multiple_of(i * 64, 64), 64), half] = oscr[lane].astype(BF16)
                 return carry
             lax.fori_loop(0, 8, line, 0)
-        copy = pltpu.make_async_copy(
-            obuf.at[pl.ds(2 * pair, 2)], out_hbm.at[pl.ds(2 * pair, 2)], out_sem.at[pair])
-        copy.start()
-        return copy
-
-    for t in range(3):
-        weights_0(t)
+
+    weights(1)
+    weights(2)
     cells_arrived(0)
     build_diffs(6, 4)
     layer_0(3)
-    weights(1)
     cells_arrived(1)
     build_diffs(4, 2)
     layer_0(2)
@@ -338,18 +367,15 @@
     cells_arrived(3)
     build_diffs(0, 2)
     layer_0(0)
-    weights(2)
     build_v(1, 1)
     layer_1(1)
     build_v(1, 0)
     layer_1(0)
     build_v(2, 2)
     build_v(2, 1)
-    out_b = layer_2(1)
+    layer_2(1)
     build_v(2, 0)
-    out_a = layer_2(0)
-    out_b.wait()
-    out_a.wait()
+    layer_2(0)
 
     for g in range(4):
         for kind in cell_kinds(g):
@@ -369,40 +395,44 @@
         any_space = pl.BlockSpec(memory_space=pl.ANY)
         decoded = pl.pallas_call(
             functools.partial(kernel, sizes),
-            out_shape=jax.ShapeDtypeStruct((4, 512, C), BF16),
+            out_shape=pltpu.VMEM((4, 512, C), BF16),
             in_specs=[any_space, any_space, pl.BlockSpec(memory_space=pltpu.VMEM)],
-            out_specs=any_space,
+            out_specs=pl.BlockSpec(memory_space=pltpu.VMEM),
             scratch_shapes=[
                 pltpu.VMEM((3, 27, C, C), BF16),
                 pltpu.VMEM((9, 3 * C, C), BF16),
                 pltpu.VMEM((2, 4, 9 * C, C), BF16),
                 pltpu.VMEM((4, 128, C), BF16),
                 pltpu.VMEM((10, 10, 16, C), BF16),
-                pltpu.VMEM((2, 10, 24, C), F32),
-                pltpu.VMEM((2, 4, 8, C), F32),
+                pltpu.VMEM((2, 10, 8, C), BF16),
+                pltpu.VMEM((2, 10, 1, C), F32),
+                pltpu.VMEM((2, 4, 8, C), BF16),
+                pltpu.VMEM((2, 4, 1, C), F32),
                 pltpu.VMEM((9, 10, 128, C), BF16),
                 pltpu.VMEM((2, 8, 18, 16, C), BF16),
                 pltpu.VMEM((2, 6, 18, 16, C), BF16),
-                pltpu.VMEM((2, 8, 32, C), F32),
-                pltpu.VMEM((2, 6, 32, C), F32),
-                pltpu.VMEM((2, 8, 16, C), F32),
-                pltpu.VMEM((2, 6, 16, C), F32),
+                pltpu.VMEM((2, 8, 16, C), BF16),
+                pltpu.VMEM((2, 6, 16, C), BF16),
+                pltpu.VMEM((2, 8, 1, C), F32),
+                pltpu.VMEM((2, 6, 1, C), F32),
+                pltpu.VMEM((2, 8, 16, C), BF16),
+                pltpu.VMEM((2, 6, 16, C), BF16),
+                pltpu.VMEM((2, 8, 1, C), F32),
+                pltpu.VMEM((2, 6, 1, C), F32),
                 pltpu.VMEM((4, 8, 288, C), BF16),
                 pltpu.VMEM((4, 6, 288, C), BF16),
                 pltpu.VMEM((9, 2, 512, 128), F32),
                 pltpu.VMEM((2, 2, 288, 128), F32),
                 pltpu.VMEM((2, 64, 128), F32),
-                pltpu.VMEM((4, 512, C), BF16),
                 pltpu.SemaphoreType.DMA,
                 pltpu.SemaphoreType.DMA((3, 3)),
-                pltpu.SemaphoreType.DMA((2,)),
                 pltpu.SemaphoreType.DMA((4, 6)),
                 pltpu.SemaphoreType.DMA((4, 6)),
                 pltpu.SemaphoreType.DMA((2, 4, 5)),
                 pltpu.SemaphoreType.DMA((2, 4, 5)),
             ],
             compiler_params=pltpu.CompilerParams(
-                collective_id=0, has_side_effects=True, vmem_limit_bytes=62 * 2**20),
+                collective_id=0, has_side_effects=True, vmem_limit_bytes=56 * 2**20),
         )(coarse.reshape(4, 128, C), kernels.reshape(3, 27, C, C), biases)
         return decoded.reshape(4, 16, 32, C)
 

time: 46.5 us -> 40.3 us (0.87)
  the two profiles are of different devices: /device:TPU:4 before, /device:TPU:6 now
where the time goes in v1:
time: 40.3 us; the launch traced here: 40 us
  Pallas kernels  39 us (97%)
  local copies, waits for them, and re-layouts  0.97 us (2%)
    pallas_call x1, Pallas kernels, local(): pl.pallas_call(functools.partial(kernel, sizes), out_shape=pltpu.VMEM((4,...  39 us
    unnamed x1, local copies, waits for them, and re-layouts  0.97 us

profile of v1, /device:TPU:6, one launch (start us, length us, event | category | flops | bytes accessed | tf_op | source)
XLA Modules:
  0.0 40.0 jit_solution(9834092302022290344)
XLA Ops:
  0.0 39.0 %shard_map.37 = bf16[4,512,256]{2,1,0:T(8,128)(2,1)S(1)} custom-call(bf16[4,128,256]{2,1,0:T(8,128)(2,1)} %bitcast.5, bf16[3,27,256,256]{3,2,1,0:T(8,128)(2,1)} %bitcast.4, f32[3,256]{1,0:T(4,128)} %bias_ref.1), custom_call_target="tpu_custom_call" | custom-call | tf_op jit(solution)/shard_map/pallas_call | solution.py:396
  39.0 1.0 %copy.5 = bf16[4,16,32,256]{3,2,1,0:T(8,128)(2,1)} copy(bf16[4,16,32,256]{3,2,1,0:T(8,128)(2,1)S(1)} %bitcast.3) | data formatting | bytes 2097152

commit v2 on v1

--- a/solution.py
+++ b/solution.py
@@ -52,7 +52,7 @@
     for copy in w_in[:3]:
         copy.start()
 
-    peers = [(dt, dr, dc) for dt in range(3) for dr in range(2) for dc in (-1, 0, 1) if (dt, dr, dc) != (0, 0, 0)]
+    peers = [(dt, dr, dc) for dt in range(2) for dr in range(2) for dc in (-1, 0, 1) if (dt, dr, dc) != (0, 0, 0)]
 
     def exists(dt, dc, sign):
         ok = True
@@ -92,18 +92,15 @@
         at = pl.ds(first, count)
         clear(cells.at[at], cell_cols.at[:, at], cell_ends.at[:, at])
 
-    @pl.when(tm < 2)
-    def _():
-        clear_frames(0, 2)
-
     @pl.when(tm < 1)
     def _():
-        clear_frames(2, 4)
+        clear_frames(0, 4)
+        clear(act2.at[:, 0:2], cols2.at[:, 0:2], ends2.at[:, 0:2])
 
     coarse_in.wait()
     for f in range(4):
         acted = silu(raw[f].astype(F32)).astype(BF16)
-        cells[6 + f, 1:9] = acted.reshape(8, 16, C)
+        cells[4 + f, 1:9] = acted.reshape(8, 16, C)
         parted(acted.astype(F32), scr, 0, pl.ds(0, 128))
         for side, x in ((0, 15), (1, 0)):
             edge = joined(scr, 0, pl.ds(x, 8, stride=16))
@@ -150,18 +147,18 @@
     for t in range(3):
         weights_0(t)
 
-    ahead = jnp.minimum(tms - 1 - tm, 2)
+    ahead = jnp.minimum(tms - 1 - tm, 1)
     beside = jnp.minimum(col, 1) + jnp.minimum(ncols - 1 - col, 1)
     pl.semaphore_wait(barrier, (1 + ahead) * 2 * (1 + beside) - 1)
 
-    groups = [(0, 0, 4, 6), (1, 2, 2, 4), (1, 0, 2, 2), (2, 2, 2, 0)]
+    groups = [(0, 0, 4, 4), (1, 2, 2, 2), (1, 0, 2, 0)]
 
     def cell_copy(g, kind):
         dt, src, count, dst = groups[g]
         if kind == 0:
-            s, d, dr, dc = cells.at[pl.ds(6 + src, count), pl.ds(1, 8)], cells.at[pl.ds(dst, count), pl.ds(1, 8)], 0, 0
+            s, d, dr, dc = cells.at[pl.ds(4 + src, count), pl.ds(1, 8)], cells.at[pl.ds(dst, count), pl.ds(1, 8)], 0, 0
         elif kind == 1:
-            s, d, dr, dc = cells.at[pl.ds(6 + src, count), 8 - 7 * row], cells.at[pl.ds(dst, count), 9 * row], 1, 0
+            s, d, dr, dc = cells.at[pl.ds(4 + src, count), 8 - 7 * row], cells.at[pl.ds(dst, count), 9 * row], 1, 0
         else:
             side = kind % 2
             dc = 1 - 2 * side
@@ -177,7 +174,7 @@
     def cell_kinds(g):
         return range(1 if groups[g][0] == 0 else 0, 6)
 
-    for g in range(4):
+    for g in range(3):
         for kind in cell_kinds(g):
             copy, there, _ = cell_copy(g, kind)
             when(there, copy.start)
@@ -192,31 +189,39 @@
 
     fine = {1: (act1, cols1, ends1, stage1, tips1), 2: (act2, cols2, ends2, stage2, tips2)}
 
-    def halo_copy(layer, pair, kind):
+    def halo_copy(layer, pair, kind, dt=0):
         act, cols, ends, stage, tips = fine[layer]
         two = pl.ds(2 * pair, 2)
-        if kind == 0:
-            s, d, dr, dc = act.at[:, two, 16 - 15 * row], act.at[:, two, 17 * row], 1, 0
+        to = pl.ds(0, 2) if dt else two
+        if kind >= 5:
+            f = kind - 5
+            s, d, dr, dc = act.at[:, 2 * pair + f, pl.ds(1, 16)], act.at[:, f, pl.ds(1, 16)], 0, 0
+        elif kind == 0:
+            s, d, dr, dc = act.at[:, two, 16 - 15 * row], act.at[:, to, 17 * row], 1, 0
         else:
             side = (kind - 1) % 2
             dc = 1 - 2 * side
             if kind < 3:
-                s, d, dr = stage.at[side, two], cols.at[side, two], 0
+                s, d, dr = stage.at[side, two], cols.at[side, to], 0
             else:
-                s, d, dr = tips.at[side, two], ends.at[side, two], 1
+                s, d, dr = tips.at[side, two], ends.at[side, to], 1
+        at = 0 if dt else pair
         copy = pltpu.make_async_remote_copy(
-            src_ref=s, dst_ref=d, send_sem=h_send.at[layer - 1, pair, kind], recv_sem=h_recv.at[layer - 1, pair, kind],
-            device_id=place(0, dr, dc, 1), device_id_type=MESH)
-        return copy, exists(0, dc, 1), exists(0, dc, -1)
-
-    def send_halos(layer, pair):
-        for kind in range(5):
-            copy, there, _ = halo_copy(layer, pair, kind)
+            src_ref=s, dst_ref=d, send_sem=h_send.at[layer - 1, at, kind], recv_sem=h_recv.at[layer - 1, at, kind],
+            device_id=place(dt, dr, dc, 1), device_id_type=MESH)
+        return copy, exists(dt, dc, 1), exists(dt, dc, -1)
+
+    spatial = {(layer, pair): [(layer, pair, kind) for kind in range(5)] for layer, pair in ((1, 0), (1, 1), (1, 2), (2, 1), (2, 2))}
+    onward = [(2, 2, kind, 1) for kind in (5, 6, 0, 1, 2, 3, 4)]
+
+    def send(copies):
+        for which in copies:
+            copy, there, _ = halo_copy(*which)
             when(there, copy.start)
 
-    def halos_arrived(layer, pair):
-        for kind in range(5):
-            copy, _, there = halo_copy(layer, pair, kind)
+    def arrived(copies):
+        for which in copies:
+            copy, _, there = halo_copy(*which)
             when(there, copy.wait_recv)
 
     def put_edge(n, first, cols, ends, side, f):
@@ -257,7 +262,7 @@
             out = [[left + (p[1] + p[0]), right + (p[1] + p[2])],
                    [left + (p[7] + p[6]), right + (p[7] + p[8])]]
             out = [[silu(v) for v in line] for line in out]
-            if pair < 2:
+            if pair < 1:
                 out = [[jnp.where(live, v, 0.0) for v in line] for line in out]
             return out
 
@@ -277,12 +282,12 @@
                         act1[px, o + f, 1 + 2 * i + py] = out[py][px].astype(BF16)
                 return carry
             lax.fori_loop(0, 8, line, 0, unroll=2)
-        send_halos(1, pair)
+        send(spatial[1, pair])
 
     def build_v(layer, pair):
         act, cols, ends, _, _ = fine[layer]
         v = v1 if layer == 1 else v2
-        halos_arrived(layer, pair)
+        arrived(spatial[layer, pair] if (layer, pair) != (2, 0) else onward)
         for f in (2 * pair, 2 * pair + 1):
             e = act[0, f].astype(F32).reshape(288, C)
             o = act[1, f].astype(F32).reshape(288, C)
@@ -296,13 +301,16 @@
             v[2, f] = (o - e).astype(BF16)
             v[3, f] = (e - joined(scr, 1, every)).astype(BF16)
 
-    def products(layer, pair):
+    def products(layer, pair, times, more=False):
         v = v1 if layer == 1 else v2
         o = 2 * pair
         for k in range(4):
             lhs = jnp.concatenate(
-                [v[k, o + t:o + t + 2, 16 * y:16 * y + 256].reshape(512, C) for t in range(3) for y in range(3)], axis=1)
-            parted(jnp.dot(lhs, u1[layer - 1, k], preferred_element_type=F32), acc, k, pl.ds(0, 512))
+                [v[k, o + t:o + t + 2, 16 * y:16 * y + 256].reshape(512, C) for t in times for y in range(3)], axis=1)
+            weight = u1[layer - 1, k, 3 * C * times[0]:3 * C * (times[-1] + 1)]
+            value = jnp.dot(lhs, weight, preferred_element_type=F32)
+            every = pl.ds(0, 512)
+            parted(value + joined(acc, k, every) if more else value, acc, k, every)
 
     def outputs(layer, at):
         bias = bias_ref[layer:layer + 1, :]
@@ -310,14 +318,11 @@
         return (m[0] + m[1]) + (m[2] + bias), (m[1] - m[2]) - (m[3] - bias)
 
     def layer_1(pair):
-        products(1, pair)
-        o = 2 * pair
+        products(1, pair, (0, 1, 2))
+        o = 2 * pair + 2
 
         def acted(at):
-            out = [silu(v) for v in outputs(1, at)]
-            if pair < 1:
-                out = [jnp.where(live, v, 0.0) for v in out]
-            return out
+            return [silu(v) for v in outputs(1, at)]
 
         for side, x in ((0, 15), (1, 0)):
             value = rounded(acted(pl.ds(x, 32, stride=16))[1 - side])
@@ -333,10 +338,10 @@
                 act2[1, o + f, two] = o_.astype(BF16).reshape(2, 16, C)
                 return carry
             lax.fori_loop(0, 8, line, 0, unroll=2)
-        send_halos(2, pair)
+        send(spatial[2, pair + 1])
 
     def layer_2(pair):
-        products(2, pair)
+        products(2, pair, (0, 1), more=True)
         for f in range(2):
             def line(i, carry, f=f):
                 e, o_ = outputs(2, pl.ds(pl.multiple_of(f * 256 + i * 32, 32), 32))
@@ -353,39 +358,36 @@
     weights(1)
     weights(2)
     cells_arrived(0)
-    build_diffs(6, 4)
-    layer_0(3)
+    build_diffs(4, 4)
+    layer_0(2)
     cells_arrived(1)
-    build_diffs(4, 2)
-    layer_0(2)
-    cells_arrived(2)
     build_diffs(2, 2)
     layer_0(1)
-    build_v(1, 3)
-    build_v(1, 2)
-    layer_1(2)
-    cells_arrived(3)
+    cells_arrived(2)
     build_diffs(0, 2)
     layer_0(0)
+    build_v(1, 2)
     build_v(1, 1)
     layer_1(1)
+    send(onward[:1])
     build_v(1, 0)
     layer_1(0)
+    send(onward[1:])
     build_v(2, 2)
+    products(2, 1, (2,))
     build_v(2, 1)
     layer_2(1)
+    products(2, 0, (2,))
     build_v(2, 0)
     layer_2(0)
 
-    for g in range(4):
+    for g in range(3):
         for kind in cell_kinds(g):
             copy, there, _ = cell_copy(g, kind)
             when(there, copy.wait_send)
-    for layer, pairs in ((1, 4), (2, 3)):
-        for pair in range(pairs):
-            for kind in range(5):
-                copy, there, _ = halo_copy(layer, pair, kind)
-                when(there, copy.wait_send)
+    for which in [*sum(spatial.values(), []), *onward]:
+        copy, there, _ = halo_copy(*which)
+        when(there, copy.wait_send)
 
 
 def solution(mesh):
@@ -403,33 +405,33 @@
                 pltpu.VMEM((9, 3 * C, C), BF16),
                 pltpu.VMEM((2, 4, 9 * C, C), BF16),
                 pltpu.VMEM((4, 128, C), BF16),
-                pltpu.VMEM((10, 10, 16, C), BF16),
-                pltpu.VMEM((2, 10, 8, C), BF16),
-                pltpu.VMEM((2, 10, 1, C), F32),
+                pltpu.VMEM((8, 10, 16, C), BF16),
+                pltpu.VMEM((2, 8, 8, C), BF16),
+                pltpu.VMEM((2, 8, 1, C), F32),
                 pltpu.VMEM((2, 4, 8, C), BF16),
                 pltpu.VMEM((2, 4, 1, C), F32),
-                pltpu.VMEM((9, 10, 128, C), BF16),
-                pltpu.VMEM((2, 8, 18, 16, C), BF16),
+                pltpu.VMEM((9, 8, 128, C), BF16),
                 pltpu.VMEM((2, 6, 18, 16, C), BF16),
-                pltpu.VMEM((2, 8, 16, C), BF16),
+                pltpu.VMEM((2, 6, 18, 16, C), BF16),
                 pltpu.VMEM((2, 6, 16, C), BF16),
-                pltpu.VMEM((2, 8, 1, C), F32),
+                pltpu.VMEM((2, 6, 16, C), BF16),
                 pltpu.VMEM((2, 6, 1, C), F32),
-                pltpu.VMEM((2, 8, 16, C), BF16),
+                pltpu.VMEM((2, 6, 1, C), F32),
                 pltpu.VMEM((2, 6, 16, C), BF16),
-                pltpu.VMEM((2, 8, 1, C), F32),
+                pltpu.VMEM((2, 6, 16, C), BF16),
                 pltpu.VMEM((2, 6, 1, C), F32),
-                pltpu.VMEM((4, 8, 288, C), BF16),
+                pltpu.VMEM((2, 6, 1, C), F32),
+                pltpu.VMEM((4, 6, 288, C), BF16),
                 pltpu.VMEM((4, 6, 288, C), BF16),
                 pltpu.VMEM((9, 2, 512, 128), F32),
                 pltpu.VMEM((2, 2, 288, 128), F32),
                 pltpu.VMEM((2, 64, 128), F32),
                 pltpu.SemaphoreType.DMA,
                 pltpu.SemaphoreType.DMA((3, 3)),
-                pltpu.SemaphoreType.DMA((4, 6)),
-                pltpu.SemaphoreType.DMA((4, 6)),
-                pltpu.SemaphoreType.DMA((2, 4, 5)),
-                pltpu.SemaphoreType.DMA((2, 4, 5)),
+                pltpu.SemaphoreType.DMA((3, 6)),
+                pltpu.SemaphoreType.DMA((3, 6)),
+                pltpu.SemaphoreType.DMA((2, 3, 7)),
+                pltpu.SemaphoreType.DMA((2, 3, 7)),
             ],
             compiler_params=pltpu.CompilerParams(
                 collective_id=0, has_side_effects=True, vmem_limit_bytes=56 * 2**20),

time: 40.3 us -> 37.7 us (0.935)
  Pallas kernels: 39 us -> 36.6 us
    pallas_call x1, Pallas kernels: 39 us -> 36.6 us  [local(): pl.pallas_call(functools.partial(kernel, sizes), out_shape=pltpu.VMEM((4,...]
where the time goes in v2:
time: 37.7 us; the launch traced here: 37.6 us
  Pallas kernels  36.6 us (97%)
  local copies, waits for them, and re-layouts  0.97 us (3%)
    pallas_call x1, Pallas kernels, local(): pl.pallas_call(functools.partial(kernel, sizes), out_shape=pltpu.VMEM((4,...  36.6 us
    unnamed x1, local copies, waits for them, and re-layouts  0.97 us

profile of v2, /device:TPU:6, one launch (start us, length us, event | category | flops | bytes accessed | tf_op | source)
XLA Modules:
  0.0 37.6 jit_solution(4715513418472448156)
XLA Ops:
  0.0 36.6 %shard_map.37 = bf16[4,512,256]{2,1,0:T(8,128)(2,1)S(1)} custom-call(bf16[4,128,256]{2,1,0:T(8,128)(2,1)} %bitcast.5, bf16[3,27,256,256]{3,2,1,0:T(8,128)(2,1)} %bitcast.4, f32[3,256]{1,0:T(4,128)} %bias_ref.1), custom_call_target="tpu_custom_call" | custom-call | tf_op jit(solution)/shard_map/pallas_call | solution.py:398
  36.6 1.0 %copy.5 = bf16[4,16,32,256]{3,2,1,0:T(8,128)(2,1)} copy(bf16[4,16,32,256]{3,2,1,0:T(8,128)(2,1)S(1)} %bitcast.3) | data formatting | bytes 2097152

commit v3 on v2

--- a/solution.py
+++ b/solution.py
@@ -123,7 +123,7 @@
                 for ky, value in enumerate((a, a + b + c, c)):
                     u0[ky * 3 + kx, to, :] = value.astype(BF16)
             return carry
-        lax.fori_loop(0, 16, chunk, 0)
+        lax.fori_loop(0, 16, chunk, 0, unroll=2)
 
     def weights(layer):
         for t in range(3):
@@ -133,19 +133,12 @@
             m, part = i // 4, i % 4
             at = pl.ds(pl.multiple_of(part * 64, 64), 64)
             to = pl.ds(pl.multiple_of(i * 64, 64), 64)
-            a = wraw[layer, 3 * m, at, :]
-            c = wraw[layer, 3 * m + 2, at, :]
-            half = 0.5 * (a.astype(F32) + c.astype(F32))
+            half = 0.5 * (wraw[layer, 3 * m, at, :].astype(F32) + wraw[layer, 3 * m + 2, at, :].astype(F32))
             b = 0.5 * wraw[layer, 3 * m + 1, at, :].astype(F32)
-            u1[layer - 1, 0, to, :] = a
-            u1[layer - 1, 1, to, :] = (half + b).astype(BF16)
-            u1[layer - 1, 2, to, :] = (half - b).astype(BF16)
-            u1[layer - 1, 3, to, :] = c
+            u1[layer - 1, 0, to, :] = (half + b).astype(BF16)
+            u1[layer - 1, 1, to, :] = (half - b).astype(BF16)
             return carry
-        lax.fori_loop(0, 36, chunk, 0)
-
-    for t in range(3):
-        weights_0(t)
+        lax.fori_loop(0, 36, chunk, 0, unroll=2)
 
     ahead = jnp.minimum(tms - 1 - tm, 1)
     beside = jnp.minimum(col, 1) + jnp.minimum(ncols - 1 - col, 1)
@@ -245,7 +238,8 @@
                 diffs[3 + kx, f] = mid.astype(BF16)
                 diffs[6 + kx, f] = (x[32:160] - mid).astype(BF16)
             return carry
-        lax.fori_loop(first, first + count, frame, 0)
+        for f in range(first, first + count):
+            frame(f, 0)
 
     live = tm > 0
 
@@ -276,12 +270,13 @@
                 tips1[side, o + f] = jnp.where(row == 0, value[15:16], value[0:1])
         for f in range(2):
             def line(i, carry, f=f):
-                out = phases(pl.ds(pl.multiple_of(f * 128 + i * 16, 16), 16))
+                out = phases(pl.ds(f * 128 + i * 16, 16))
                 for py in range(2):
                     for px in range(2):
                         act1[px, o + f, 1 + 2 * i + py] = out[py][px].astype(BF16)
                 return carry
-            lax.fori_loop(0, 8, line, 0, unroll=2)
+            for i in range(8):
+                line(i, 0)
         send(spatial[1, pair])
 
     def build_v(layer, pair):
@@ -307,7 +302,11 @@
         for k in range(4):
             lhs = jnp.concatenate(
                 [v[k, o + t:o + t + 2, 16 * y:16 * y + 256].reshape(512, C) for t in times for y in range(3)], axis=1)
-            weight = u1[layer - 1, k, 3 * C * times[0]:3 * C * (times[-1] + 1)]
+            if k in (1, 2):
+                weight = u1[layer - 1, k - 1, 3 * C * times[0]:3 * C * (times[-1] + 1)]
+            else:
+                weight = jnp.concatenate(
+                    [wraw[layer, 3 * (3 * t + y) + 2 * (k // 3)] for t in times for y in range(3)], axis=0)
             value = jnp.dot(lhs, weight, preferred_element_type=F32)
             every = pl.ds(0, 512)
             parted(value + joined(acc, k, every) if more else value, acc, k, every)
@@ -332,31 +331,34 @@
                 tips2[side, o + f] = jnp.where(row == 0, line[15:16], line[0:1])
         for f in range(2):
             def line(i, carry, f=f):
-                e, o_ = acted(pl.ds(pl.multiple_of(f * 256 + i * 32, 32), 32))
+                e, o_ = acted(pl.ds(f * 256 + i * 32, 32))
                 two = pl.ds(1 + 2 * i, 2)
                 act2[0, o + f, two] = e.astype(BF16).reshape(2, 16, C)
                 act2[1, o + f, two] = o_.astype(BF16).reshape(2, 16, C)
                 return carry
-            lax.fori_loop(0, 8, line, 0, unroll=2)
+            for i in range(8):
+                line(i, 0)
         send(spatial[2, pair + 1])
 
     def layer_2(pair):
-        products(2, pair, (0, 1), more=True)
         for f in range(2):
             def line(i, carry, f=f):
-                e, o_ = outputs(2, pl.ds(pl.multiple_of(f * 256 + i * 32, 32), 32))
-                up = raw[2 * pair + f, pl.ds(pl.multiple_of(i * 16, 16), 16), :].astype(F32)
+                e, o_ = outputs(2, pl.ds(f * 256 + i * 32, 32))
+                up = raw[2 * pair + f, pl.ds(i * 16, 16), :].astype(F32)
                 up = jnp.concatenate([up, up], axis=0)
                 for lane in range(2):
                     half = slice(128 * lane, 128 * lane + 128)
-                    oscr[lane, pl.ds(0, 32, stride=2), :] = (up + e)[:, half]
-                    oscr[lane, pl.ds(1, 32, stride=2), :] = (up + o_)[:, half]
-                    obuf[2 * pair + f, pl.ds(pl.multiple_of(i * 64, 64), 64), half] = oscr[lane].astype(BF16)
+                    oscr[i, lane, pl.ds(0, 32, stride=2), :] = (up + e)[:, half]
+                    oscr[i, lane, pl.ds(1, 32, stride=2), :] = (up + o_)[:, half]
+                    obuf[2 * pair + f, pl.ds(i * 64, 64), half] = oscr[i, lane].astype(BF16)
                 return carry
-            lax.fori_loop(0, 8, line, 0)
-
+            for i in range(8):
+                line(i, 0)
+
+    weights_0(0)
+    weights_0(1)
+    weights_0(2)
     weights(1)
-    weights(2)
     cells_arrived(0)
     build_diffs(4, 4)
     layer_0(2)
@@ -373,12 +375,14 @@
     build_v(1, 0)
     layer_1(0)
     send(onward[1:])
+    weights(2)
     build_v(2, 2)
-    products(2, 1, (2,))
     build_v(2, 1)
+    products(2, 1, (0, 1, 2))
     layer_2(1)
     products(2, 0, (2,))
     build_v(2, 0)
+    products(2, 0, (0, 1), more=True)
     layer_2(0)
 
     for g in range(3):
@@ -403,7 +407,7 @@
             scratch_shapes=[
                 pltpu.VMEM((3, 27, C, C), BF16),
                 pltpu.VMEM((9, 3 * C, C), BF16),
-                pltpu.VMEM((2, 4, 9 * C, C), BF16),
+                pltpu.VMEM((2, 2, 9 * C, C), BF16),
                 pltpu.VMEM((4, 128, C), BF16),
                 pltpu.VMEM((8, 10, 16, C), BF16),
                 pltpu.VMEM((2, 8, 8, C), BF16),
@@ -425,7 +429,7 @@
                 pltpu.VMEM((4, 6, 288, C), BF16),
                 pltpu.VMEM((9, 2, 512, 128), F32),
                 pltpu.VMEM((2, 2, 288, 128), F32),
-                pltpu.VMEM((2, 64, 128), F32),
+                pltpu.VMEM((8, 2, 64, 128), F32),
                 pltpu.SemaphoreType.DMA,
                 pltpu.SemaphoreType.DMA((3, 3)),
                 pltpu.SemaphoreType.DMA((3, 6)),

time: 37.7 us -> 34.8 us (0.923)
  Pallas kernels: 36.6 us -> 33.7 us
    pallas_call x1, Pallas kernels: 36.6 us -> 33.7 us  [local(): pl.pallas_call(functools.partial(kernel, sizes), out_shape=pltpu.VMEM((4,...]
where the time goes in v3:
time: 34.8 us; the launch traced here: 34.7 us
  Pallas kernels  33.7 us (97%)
  local copies, waits for them, and re-layouts  0.97 us (3%)
    pallas_call x1, Pallas kernels, local(): pl.pallas_call(functools.partial(kernel, sizes), out_shape=pltpu.VMEM((4,...  33.7 us
    unnamed x1, local copies, waits for them, and re-layouts  0.97 us

profile of v3, /device:TPU:6, one launch (start us, length us, event | category | flops | bytes accessed | tf_op | source)
XLA Modules:
  0.0 34.7 jit_solution(2266412536850771057)
XLA Ops:
  0.0 33.7 %shard_map.37 = bf16[4,512,256]{2,1,0:T(8,128)(2,1)S(1)} custom-call(bf16[4,128,256]{2,1,0:T(8,128)(2,1)} %bitcast.5, bf16[3,27,256,256]{3,2,1,0:T(8,128)(2,1)} %bitcast.4, f32[3,256]{1,0:T(4,128)} %bias_ref.1), custom_call_target="tpu_custom_call" | custom-call | tf_op jit(solution)/shard_map/pallas_call | solution.py:402
  33.7 1.0 %copy.5 = bf16[4,16,32,256]{3,2,1,0:T(8,128)(2,1)} copy(bf16[4,16,32,256]{3,2,1,0:T(8,128)(2,1)S(1)} %bitcast.3) | data formatting | bytes 2097152

commit v4 on v3

--- a/solution.py
+++ b/solution.py
@@ -205,7 +205,7 @@
         return copy, exists(dt, dc, 1), exists(dt, dc, -1)
 
     spatial = {(layer, pair): [(layer, pair, kind) for kind in range(5)] for layer, pair in ((1, 0), (1, 1), (1, 2), (2, 1), (2, 2))}
-    onward = [(2, 2, kind, 1) for kind in (5, 6, 0, 1, 2, 3, 4)]
+    onward = [(2, 2, kind, 1) for kind in (5, 0, 1, 2, 3, 4, 6)]
 
     def send(copies):
         for which in copies:
@@ -279,11 +279,14 @@
                 line(i, 0)
         send(spatial[1, pair])
 
-    def build_v(layer, pair):
+    def build_v(layer, pair, frames=(0, 1)):
         act, cols, ends, _, _ = fine[layer]
         v = v1 if layer == 1 else v2
-        arrived(spatial[layer, pair] if (layer, pair) != (2, 0) else onward)
-        for f in (2 * pair, 2 * pair + 1):
+        if (layer, pair) != (2, 0):
+            arrived(spatial[layer, pair])
+        else:
+            arrived(onward[:6] if 0 in frames else onward[6:])
+        for f in (2 * pair + f for f in frames):
             e = act[0, f].astype(F32).reshape(288, C)
             o = act[1, f].astype(F32).reshape(288, C)
             every = pl.ds(0, 288)
@@ -296,19 +299,20 @@
             v[2, f] = (o - e).astype(BF16)
             v[3, f] = (e - joined(scr, 1, every)).astype(BF16)
 
-    def products(layer, pair, times, more=False):
+    def products(layer, pair, times, more=False, frames=(0, 1)):
         v = v1 if layer == 1 else v2
-        o = 2 * pair
+        o, first, rows_ = 2 * pair, frames[0], 256 * len(frames)
         for k in range(4):
             lhs = jnp.concatenate(
-                [v[k, o + t:o + t + 2, 16 * y:16 * y + 256].reshape(512, C) for t in times for y in range(3)], axis=1)
+                [v[k, o + t + first:o + t + first + len(frames), 16 * y:16 * y + 256].reshape(rows_, C)
+                 for t in times for y in range(3)], axis=1)
             if k in (1, 2):
                 weight = u1[layer - 1, k - 1, 3 * C * times[0]:3 * C * (times[-1] + 1)]
             else:
                 weight = jnp.concatenate(
                     [wraw[layer, 3 * (3 * t + y) + 2 * (k // 3)] for t in times for y in range(3)], axis=0)
             value = jnp.dot(lhs, weight, preferred_element_type=F32)
-            every = pl.ds(0, 512)
+            every = pl.ds(256 * first, rows_)
             parted(value + joined(acc, k, every) if more else value, acc, k, every)
 
     def outputs(layer, at):
@@ -317,7 +321,6 @@
         return (m[0] + m[1]) + (m[2] + bias), (m[1] - m[2]) - (m[3] - bias)
 
     def layer_1(pair):
-        products(1, pair, (0, 1, 2))
         o = 2 * pair + 2
 
         def acted(at):
@@ -362,6 +365,7 @@
     cells_arrived(0)
     build_diffs(4, 4)
     layer_0(2)
+    weights(2)
     cells_arrived(1)
     build_diffs(2, 2)
     layer_0(1)
@@ -369,20 +373,27 @@
     build_diffs(0, 2)
     layer_0(0)
     build_v(1, 2)
+    products(1, 1, (2,))
     build_v(1, 1)
+    products(1, 1, (0, 1), more=True)
     layer_1(1)
-    send(onward[:1])
+    send(onward[:6])
     build_v(1, 0)
+    products(1, 0, (0, 1, 2))
     layer_1(0)
-    send(onward[1:])
-    weights(2)
+    send(onward[6:])
     build_v(2, 2)
+    products(2, 1, (2,))
     build_v(2, 1)
-    products(2, 1, (0, 1, 2))
+    products(2, 1, (0, 1), more=True)
     layer_2(1)
-    products(2, 0, (2,))
-    build_v(2, 0)
-    products(2, 0, (0, 1), more=True)
+    products(2, 0, (2,), frames=(0,))
+    products(2, 0, (1, 2), frames=(1,))
+    build_v(2, 0, (0,))
+    products(2, 0, (0,), more=True, frames=(0,))
+    build_v(2, 0, (1,))
+    products(2, 0, (1,), more=True, frames=(0,))
+    products(2, 0, (0,), more=True, frames=(1,))
     layer_2(0)
 
     for g in range(3):

time: 34.8 us -> 33.5 us (0.963)
  Pallas kernels: 33.7 us -> 32.3 us
    pallas_call x1, Pallas kernels: 33.7 us -> 32.3 us  [local(): pl.pallas_call(functools.partial(kernel, sizes), out_shape=pltpu.VMEM((4,...]
where the time goes in v4:
time: 33.5 us; the launch traced here: 33.3 us
  Pallas kernels  32.3 us (96%)
  local copies, waits for them, and re-layouts  0.97 us (3%)
    pallas_call x1, Pallas kernels, local(): pl.pallas_call(functools.partial(kernel, sizes), out_shape=pltpu.VMEM((4,...  32.3 us
    unnamed x1, local copies, waits for them, and re-layouts  0.97 us

profile of v4, /device:TPU:6, one launch (start us, length us, event | category | flops | bytes accessed | tf_op | source)
XLA Modules:
  0.0 33.3 jit_solution(7880878144052416868)
XLA Ops:
  0.0 32.3 %shard_map.37 = bf16[4,512,256]{2,1,0:T(8,128)(2,1)S(1)} custom-call(bf16[4,128,256]{2,1,0:T(8,128)(2,1)} %bitcast.5, bf16[3,27,256,256]{3,2,1,0:T(8,128)(2,1)} %bitcast.4, f32[3,256]{1,0:T(4,128)} %bias_ref.1), custom_call_target="tpu_custom_call" | custom-call | tf_op jit(solution)/shard_map/pallas_call | solution.py:413
  32.4 1.0 %copy.5 = bf16[4,16,32,256]{3,2,1,0:T(8,128)(2,1)} copy(bf16[4,16,32,256]{3,2,1,0:T(8,128)(2,1)S(1)} %bitcast.3) | data formatting | bytes 2097152

commit v5 on v4

--- a/solution.py
+++ b/solution.py
@@ -101,9 +101,9 @@
     for f in range(4):
         acted = silu(raw[f].astype(F32)).astype(BF16)
         cells[4 + f, 1:9] = acted.reshape(8, 16, C)
-        parted(acted.astype(F32), scr, 0, pl.ds(0, 128))
+        parted(acted.astype(F32), scr, f, pl.ds(0, 128))
         for side, x in ((0, 15), (1, 0)):
-            edge = joined(scr, 0, pl.ds(x, 8, stride=16))
+            edge = joined(scr, f, pl.ds(x, 8, stride=16))
             cell_stage[side, f] = edge.astype(BF16)
             cell_tips[side, f] = jnp.where(row == 0, edge[7:8], edge[0:1])
 
@@ -227,12 +227,12 @@
     def build_diffs(first, count):
         def frame(f, carry):
             c = cells[f].astype(F32).reshape(160, C)
-            every = pl.ds(0, 160)
-            parted(pltpu.roll(c, 1, 0), scr, 0, every)
-            put_edge(0, 0, cell_cols, cell_ends, 0, f)
-            parted(pltpu.roll(c, 159, 0), scr, 1, every)
-            put_edge(1, 15, cell_cols, cell_ends, 1, f)
-            for kx, x in enumerate((joined(scr, 0, every) - c, c, joined(scr, 1, every) - c)):
+            every, n = pl.ds(0, 160), 2 * (f % 2)
+            parted(pltpu.roll(c, 1, 0), scr, n, every)
+            put_edge(n, 0, cell_cols, cell_ends, 0, f)
+            parted(pltpu.roll(c, 159, 0), scr, n + 1, every)
+            put_edge(n + 1, 15, cell_cols, cell_ends, 1, f)
+            for kx, x in enumerate((joined(scr, n, every) - c, c, joined(scr, n + 1, every) - c)):
                 mid = x[16:144]
                 diffs[kx, f] = (x[0:128] - mid).astype(BF16)
                 diffs[3 + kx, f] = mid.astype(BF16)
@@ -263,9 +263,9 @@
         for side, x in ((0, 15), (1, 0)):
             edge = phases(pl.ds(x, 16, stride=16))
             for py in range(2):
-                parted(rounded(edge[py][1 - side]), scr, 0, pl.ds(py, 16, stride=2))
+                parted(rounded(edge[py][1 - side]), scr, side, pl.ds(py, 16, stride=2))
             for f in range(2):
-                value = joined(scr, 0, pl.ds(16 * f, 16))
+                value = joined(scr, side, pl.ds(16 * f, 16))
                 stage1[side, o + f] = value.astype(BF16)
                 tips1[side, o + f] = jnp.where(row == 0, value[15:16], value[0:1])
         for f in range(2):
@@ -289,15 +289,15 @@
         for f in (2 * pair + f for f in frames):
             e = act[0, f].astype(F32).reshape(288, C)
             o = act[1, f].astype(F32).reshape(288, C)
-            every = pl.ds(0, 288)
-            parted(pltpu.roll(o, 1, 0), scr, 0, every)
-            put_edge(0, 0, cols, ends, 0, f)
-            parted(pltpu.roll(e, 287, 0), scr, 1, every)
-            put_edge(1, 15, cols, ends, 1, f)
-            v[0, f] = (joined(scr, 0, every) - o).astype(BF16)
+            every, n = pl.ds(0, 288), 2 * (f % 2)
+            parted(pltpu.roll(o, 1, 0), scr, n, every)
+            put_edge(n, 0, cols, ends, 0, f)
+            parted(pltpu.roll(e, 287, 0), scr, n + 1, every)
+            put_edge(n + 1, 15, cols, ends, 1, f)
+            v[0, f] = (joined(scr, n, every) - o).astype(BF16)
             v[1, f] = (e + o).astype(BF16)
             v[2, f] = (o - e).astype(BF16)
-            v[3, f] = (e - joined(scr, 1, every)).astype(BF16)
+            v[3, f] = (e - joined(scr, n + 1, every)).astype(BF16)
 
     def products(layer, pair, times, more=False, frames=(0, 1)):
         v = v1 if layer == 1 else v2
@@ -439,7 +439,7 @@
                 pltpu.VMEM((4, 6, 288, C), BF16),
                 pltpu.VMEM((4, 6, 288, C), BF16),
                 pltpu.VMEM((9, 2, 512, 128), F32),
-                pltpu.VMEM((2, 2, 288, 128), F32),
+                pltpu.VMEM((4, 2, 288, 128), F32),
                 pltpu.VMEM((8, 2, 64, 128), F32),
                 pltpu.SemaphoreType.DMA,
                 pltpu.SemaphoreType.DMA((3, 3)),

time: 33.5 us -> 33.5 us (level)
  no operation moved by 1% of the time
where the time goes in v5:
time: 33.5 us; the launch traced here: 33.4 us
  Pallas kernels  32.4 us (97%)
  local copies, waits for them, and re-layouts  0.97 us (3%)
    pallas_call x1, Pallas kernels, local(): pl.pallas_call(functools.partial(kernel, sizes), out_shape=pltpu.VMEM((4,...  32.4 us
    unnamed x1, local copies, waits for them, and re-layouts  0.97 us

profile of v5, /device:TPU:6, one launch (start us, length us, event | category | flops | bytes accessed | tf_op | source)
XLA Modules:
  0.0 33.4 jit_solution(18192998038551086238)
XLA Ops:
  0.0 32.4 %shard_map.37 = bf16[4,512,256]{2,1,0:T(8,128)(2,1)S(1)} custom-call(bf16[4,128,256]{2,1,0:T(8,128)(2,1)} %bitcast.5, bf16[3,27,256,256]{3,2,1,0:T(8,128)(2,1)} %bitcast.4, f32[3,256]{1,0:T(4,128)} %bias_ref.1), custom_call_target="tpu_custom_call" | custom-call | tf_op jit(solution)/shard_map/pallas_call | solution.py:413
  32.4 1.0 %copy.5 = bf16[4,16,32,256]{3,2,1,0:T(8,128)(2,1)} copy(bf16[4,16,32,256]{3,2,1,0:T(8,128)(2,1)S(1)} %bitcast.3) | data formatting | bytes 2097152
